TPU v7x, 128 devices: a whole 4x4x4 slice. The times are simulated.
128 devices in a mesh: grp: 4 (over z), list: 32 (over y, x, core).
Axes of the slice: x: 4, y: 4, z: 4, core: 2. Of those that a mesh axis runs over, the one named last changes fastest.
Arguments:
- vectors: bfloat16 [3, 65536, 1024], P(None, ('grp', 'list')), may hold values from -6 to 6
- owner_route: int32 [3, 65536, 1], P(None, ('grp', 'list')), may hold values from 0 to 31; in each aligned block of 512 rows (0 to 511, 512 to 1023, ..., all dimensions but the last counted through in order) at most 32 rows name the same one
- list_slot: int32 [3, 65536], P(None, ('grp', 'list')), may hold values from 0 to 1023
- centroids: float32 [32768, 1024], P('list'), may hold values from -6 to 6
- counts: int32 [32768], P('list'), may hold values from 1 to 8
Outputs:
- residuals: bfloat16 [3, 65536, 1024], P(None, ('grp', 'list'))
- new_centroids: float32 [32768, 1024], P('list')
Inputs may be any that keep to these rules, and one draw needn't show every extreme that they name: `owner_route`: within the rows of one device for one step, at most 32 vectors name the same owner; some owner is named exactly 32 times.
All inputs are finite; a program needn't handle non-finite values.
Results may differ from a plain program's by a relative error of at most 0.0035.
Values may be sent and summed in bfloat16 or wider, within the bound.
No kernel may reach another device: no remote copies, remote signals or barrier semaphores. Data moves between devices by JAX's collectives and lax.ppermute only.
A program may use at most 128 MiB of HBM per device.

v0:
```python
import jax
import jax.numpy as jnp
from jax import lax
from jax.sharding import PartitionSpec as P

STEPS = 3


def tie(value, *others):
    return lax.optimization_barrier((value,) + others)[0]


def split_table(table):
    hi = lax.reduce_precision(table, 8, 7)
    lo = table - hi
    return jnp.concatenate([hi.astype(jnp.bfloat16), lo.astype(jnp.bfloat16)], axis=0)


def local(vectors, owner_route, list_slot, centroids, counts):
    owner_count = lax.axis_size("list")
    grp_count = lax.axis_size("grp")
    row_count = vectors.shape[1]
    width = vectors.shape[2]
    capacity = 2 * row_count // owner_count
    list_dev = centroids.shape[0]
    total_rows = owner_count * capacity
    owner_ids = owner_route[:, :, 0]
    hits = owner_ids[:, :, None] == jnp.arange(owner_count, dtype=jnp.int32)
    earlier = jnp.arange(row_count)[:, None] > jnp.arange(row_count)[None, :]
    before = jnp.einsum(
        "ij,sjo->sio",
        earlier.astype(jnp.bfloat16),
        hits.astype(jnp.bfloat16),
        preferred_element_type=jnp.float32,
    )
    rank = jnp.sum(jnp.where(hits, before, 0.0), axis=2).astype(jnp.int32)
    dest = owner_ids * capacity + rank
    row_iota = jnp.arange(total_rows, dtype=jnp.int32)
    place = dest[:, None, :] == row_iota[None, :, None]
    slots = jnp.sum(jnp.where(place, list_slot[:, None, :] + 1, 0), axis=2) - 1
    slots = slots.reshape(STEPS, owner_count, capacity).transpose(1, 0, 2)
    slots = slots.reshape(owner_count, 1, STEPS * capacity)
    slots = lax.all_to_all(slots, "list", split_axis=0, concat_axis=0, tiled=True)
    slots = slots.reshape(owner_count, STEPS, capacity).transpose(1, 0, 2)
    slots = slots.reshape(STEPS, total_rows)
    list_iota = jnp.arange(list_dev, dtype=jnp.int32)
    batch = jnp.sum((slots[:, None, :] == list_iota[None, :, None]).astype(jnp.int32), axis=2)
    parts = [batch]
    for offset in range(1, grp_count):
        parts.append(
            lax.ppermute(batch, "grp", [(i, (i + offset) % grp_count) for i in range(grp_count)])
        )
    batch = sum(parts).astype(jnp.float32)

    def exchange(rows):
        rows = rows.reshape(owner_count, capacity, width)
        rows = lax.all_to_all(rows, "list", split_axis=0, concat_axis=0, tiled=True)
        return rows.reshape(total_rows, width)

    received = []
    for step in range(STEPS):
        send = jnp.dot(
            (dest[step][None, :] == row_iota[:, None]).astype(jnp.bfloat16),
            vectors[step],
            preferred_element_type=jnp.float32,
        ).astype(jnp.bfloat16)
        if received:
            send = tie(send, received[-1])
        received.append(exchange(send))
    totals = []
    for step in range(STEPS):
        one_hot = (list_iota[:, None] == slots[step][None, :]).astype(jnp.bfloat16)
        sums = jnp.dot(one_hot, received[step], preferred_element_type=jnp.float32)
        sums = sums.astype(jnp.bfloat16)
        if totals:
            sums = tie(sums, totals[-1])
        totals.append(lax.psum(sums, "grp"))
    weights = counts.astype(jnp.float32)
    mass = weights[:, None] * centroids
    current = centroids
    outputs = []
    last = received[-1]
    backs = []
    for step in range(STEPS):
        one_hot = (
            slots[step][:, None] == (jnp.arange(2 * list_dev, dtype=jnp.int32) % list_dev)[None, :]
        )
        chosen = jnp.dot(
            one_hot.astype(jnp.bfloat16), split_table(current), preferred_element_type=jnp.float32
        )
        residual = (received[step].astype(jnp.float32) - chosen).astype(jnp.bfloat16)
        back = exchange(tie(residual, last))
        last = back
        backs.append(back)
        pick = (dest[step][:, None] == row_iota[None, :]).astype(jnp.bfloat16)
        outputs.append(jnp.dot(pick, back, preferred_element_type=jnp.float32).astype(jnp.bfloat16))
        total = tie(totals[step], received[-1] if step == 0 else backs[-2])
        mass = mass + total.astype(jnp.float32)
        weights = weights + batch[step]
        current = mass / weights[:, None]
    return (jnp.stack(outputs, axis=0), current)


def solution(mesh):
    in_specs = (
        P(None, ("grp", "list"), None),
        P(None, ("grp", "list"), None),
        P(None, ("grp", "list")),
        P("list", None),
        P("list"),
    )
    out_specs = (P(None, ("grp", "list"), None), P("list", None))
    return jax.shard_map(local, mesh=mesh, in_specs=in_specs, out_specs=out_specs, check_vma=False)
```

profile of v0, /device:TPU:0, one launch (start us, length us, event | category | flops | bytes accessed | tf_op | source)
XLA Modules:
  0.0 316.4 jit_solution(11587762332282311893)
XLA Ops:
  7.2 0.7 copy.20
  7.9 0.3 fusion.62
  8.2 0.7 convert_add_fusion.2
  8.9 3.8 %fusion.39 = bf16[1024,1024]{1,0:T(8,128)(2,1)} fusion(bf16[3,512,1024]{2,1,0:T(8,128)(2,1)} %param.5, s32[512]{0:T(512)S(1)} %bitcast.76), kind=kOutput, calls=%fused_computation.66 | convolution fusion | flops 1075314688 | bytes 3147776 | tf_op jit(solution)/shard_map/dot_general | solution.py:62
  12.7 7.4 %all-to-all-start = ((bf16[32,32,1024]{2,1,0:T(8,128)(2,1)}), bf16[32,32,1024]{2,1,0:T(8,128)(2,1)S(1)}, u32[]{:S(2)}, u32[]{:S(2)}) async-start(bf16[32,32,1024]{2,1,0:T(8,128)(2,1)} %bitcast.63), calls=%async_computation | async-start | bytes 4194304 | tf_op jit(solution)/shard_map/all_to_all | solution.py:57
  20.1 0.8 select_reduce_fusion
  20.9 0.1 sub.25
  21.1 0.7 reshape.93
  21.8 28.3 %all-to-all-done = bf16[32,32,1024]{2,1,0:T(8,128)(2,1)S(1)} async-done(((bf16[32,32,1024]{2,1,0:T(8,128)(2,1)}), bf16[32,32,1024]{2,1,0:T(8,128)(2,1)S(1)}, u32[]{:S(2)}, u32[]{:S(2)}) %all-to-all-start) | async-done | bytes 2097184 | tf_op jit(solution)/shard_map/all_to_all | solution.py:57
  50.1 3.8 %all-to-all-start.1 = ((s32[32,1,96]{2,1,0:T(1,128)}), s32[32,1,96]{2,1,0:T(1,128)S(1)}, u32[]{:S(2)}, u32[]{:S(2)}) async-start(s32[32,1,96]{2,1,0:T(1,128)} %bitcast.7), calls=%async_computation.1 | async-start | bytes 32768 | tf_op jit(solution)/shard_map/all_to_all | solution.py:43
  53.9 3.8 %fusion.37 = bf16[1024,1024]{1,0:T(8,128)(2,1)} fusion(bf16[3,512,1024]{2,1,0:T(8,128)(2,1)} %param.5, s32[512]{0:T(512)S(1)} %bitcast.74), kind=kOutput, calls=%fused_computation.64 | convolution fusion | flops 1075314688 | bytes 3147776 | tf_op jit(solution)/shard_map/dot_general | solution.py:62
  57.7 3.5 %all-to-all-done.1 = s32[32,1,96]{2,1,0:T(1,128)S(1)} async-done(((s32[32,1,96]{2,1,0:T(1,128)}), s32[32,1,96]{2,1,0:T(1,128)S(1)}, u32[]{:S(2)}, u32[]{:S(2)}) %all-to-all-start.1) | async-done | bytes 12320 | tf_op jit(solution)/shard_map/all_to_all | solution.py:43
  61.2 4.8 %all-to-all-start.2 = ((bf16[32,32,1024]{2,1,0:T(8,128)(2,1)}), bf16[32,32,1024]{2,1,0:T(8,128)(2,1)}, u32[]{:S(2)}, u32[]{:S(2)}) async-start(bf16[32,32,1024]{2,1,0:T(8,128)(2,1)} %bitcast.60), calls=%async_computation.2 | async-start | bytes 4194304 | tf_op jit(solution)/shard_map/all_to_all | solution.py:57
  66.0 0.0 all-reduce.4.cloned.1.call-start
  66.0 0.5 broadcast.53
  66.5 0.7 reduce.15
  67.2 0.1 reshape.94
  67.3 0.1 slice_reduce_fusion
  67.5 0.1 eq.226
  67.5 3.7 %fusion.42 = bf16[1024,1024]{1,0:T(8,128)(2,1)} fusion(bf16[1024,1024]{1,0:T(8,128)(2,1)S(1)} %bitcast.56, s32[1024]{0:T(1024)S(1)} %eq.226), kind=kOutput, calls=%fused_computation.69 | convolution fusion | flops 2149580800 | bytes 4198400 | tf_op jit(solution)/shard_map/dot_general | solution.py:73
  71.2 0.0 all-reduce.4.cloned.1.call-update
  71.2 3.8 %fusion.38 = bf16[1024,1024]{1,0:T(8,128)(2,1)} fusion(bf16[3,512,1024]{2,1,0:T(8,128)(2,1)} %param.5, s32[512]{0:T(512)S(1)} %bitcast.72), kind=kOutput, calls=%fused_computation.65 | convolution fusion | flops 1075314688 | bytes 3147776 | tf_op jit(solution)/shard_map/dot_general | solution.py:62
  75.0 0.0 copy-start
  75.0 20.9 %all-to-all-done.2 = bf16[32,32,1024]{2,1,0:T(8,128)(2,1)} async-done(((bf16[32,32,1024]{2,1,0:T(8,128)(2,1)}), bf16[32,32,1024]{2,1,0:T(8,128)(2,1)}, u32[]{:S(2)}, u32[]{:S(2)}) %all-to-all-start.2) | async-done | bytes 2097184 | tf_op jit(solution)/shard_map/all_to_all | solution.py:57
  95.9 4.8 %all-to-all-start.3 = ((bf16[32,32,1024]{2,1,0:T(8,128)(2,1)}), bf16[32,32,1024]{2,1,0:T(8,128)(2,1)}, u32[]{:S(2)}, u32[]{:S(2)}) async-start(bf16[32,32,1024]{2,1,0:T(8,128)(2,1)} %bitcast.58), calls=%async_computation.3 | async-start | bytes 4194304 | tf_op jit(solution)/shard_map/all_to_all | solution.py:57
  100.7 0.0 all-reduce.6.cloned.1.call-start
  100.8 0.1 eq.247
  100.9 1.5 convert_reduce_fusion
  102.4 4.1 %collective-permute-start.2 = (s32[3,1024]{1,0:T(4,128)S(1)}, s32[3,1024]{1,0:T(4,128)S(1)}, u32[]{:S(2)}, u32[]{:S(2)}) collective-permute-start(s32[3,1024]{1,0:T(4,128)S(1)} %convert_reduce_fusion), channel_id=1, source_target_pairs={{0,96},{32,0},{64,32},{96,64},{1,97},{33,1},{65,33},{97,65},{2,98}... | collective-permute-start | bytes 36872 | tf_op jit(solution)/shard_map/ppermute | solution.py:51
  106.5 0.0 collective-permute-start.1
  106.5 1.3 collective-permute-start
  107.8 0.0 copy-done
  107.8 0.1 eq.241
  107.9 0.1 eq.254
  107.9 0.0 collective-permute-done.2
  108.0 3.8 %collective-permute-done.1 = s32[3,1024]{1,0:T(4,128)S(1)} collective-permute-done((s32[3,1024]{1,0:T(4,128)S(1)}, s32[3,1024]{1,0:T(4,128)S(1)}, u32[]{:S(2)}, u32[]{:S(2)}) %collective-permute-start.1) | collective-permute-done | bytes 12320 | tf_op jit(solution)/shard_map/ppermute | solution.py:51
  111.8 0.0 collective-permute-done
  111.8 5.4 %fusion.41 = bf16[1024,1024]{1,0:T(8,128)(2,1)} fusion(bf16[1024,1024]{1,0:T(8,128)(2,1)} %bitcast.14, s32[1024]{0:T(1024)S(1)} %eq.241), kind=kOutput, calls=%fused_computation.68 | convolution fusion | flops 2149580800 | bytes 4198400 | tf_op jit(solution)/shard_map/dot_general | solution.py:73
  117.2 15.5 %all-reduce.4.cloned.1.call-done = bf16[1024,1024]{1,0:T(8,128)(2,1)} async-done(((bf16[1024,1024]{1,0:T(8,128)(2,1)}), bf16[1024,1024]{1,0:T(8,128)(2,1)}) %all-reduce.4.cloned.1.call-update) | async-done | bytes 2097168 | tf_op jit(solution)/shard_map/psum | solution.py:77
  132.7 0.0 all-reduce.6.cloned.1.call-update
  132.8 0.0 all-to-all-done.3
  132.8 5.3 %reduce-precision_convert_fusion.1 = (bf16[1024,1024]{1,0:T(8,128)(2,1)}, f32[1024,1024]{1,0:T(8,128)}, bf16[1024,1024]{1,0:T(8,128)(2,1)S(1)}, bf16[1024,1024]{1,0:T(8,128)(2,1)S(1)}) fusion(f32[1024]{0:T(1024)S(1)} %get-tuple-element.27, bf16[1024,1024]{1,0:T(8,128)(2,1)} %all-reduce.4.cloned.1.call-done, f32[1024,1024]{1,0:T(8,128)} %param.8, ...), kind=kLoop, calls=%fused_computation.13 | loop fusion | flops 10485760 | bytes 16785408 | tf_op jit(solution)/shard_map/convert_element_type | solution.py:16
  138.1 5.9 %subtract_convert_fusion.2 = bf16[1024,1024]{1,0:T(8,128)(2,1)} fusion(bf16[1024,1024]{1,0:T(8,128)(2,1)S(1)} %bitcast.57, bf16[1024,1024]{1,0:T(8,128)(2,1)S(1)} %get-tuple-element.34, bf16[1024,1024]{1,0:T(8,128)(2,1)S(1)} %get-tuple-element.33, s32[2048]{0:T(1024)S(1)} %add_select_fusion, s32[1024]{0:T(1024)S(1)} %eq.226), kind=kOutput, calls=%fused_computation.36 | convolution fusion | flops 4308598784 | bytes 8400896 | tf_op jit(solution)/shard_map/dot_general | solution.py:88
  144.0 7.1 %all-to-all-start.4 = ((bf16[32,32,1024]{2,1,0:T(8,128)(2,1)}), bf16[32,32,1024]{2,1,0:T(8,128)(2,1)S(1)}, u32[]{:S(2)}, u32[]{:S(2)}) async-start(bf16[32,32,1024]{2,1,0:T(8,128)(2,1)} %bitcast.61), calls=%async_computation.4 | async-start | bytes 4194304 | tf_op jit(solution)/shard_map/all_to_all | solution.py:57
  151.1 0.3 all-reduce.8.cloned.1.call-start
  151.4 5.3 %fusion.40 = bf16[1024,1024]{1,0:T(8,128)(2,1)} fusion(bf16[1024,1024]{1,0:T(8,128)(2,1)} %bitcast.16, s32[1024]{0:T(1024)S(1)} %eq.254), kind=kOutput, calls=%fused_computation.67 | convolution fusion | flops 2149580800 | bytes 4198400 | tf_op jit(solution)/shard_map/dot_general | solution.py:73
  156.7 4.4 %fusion.7 = bf16[1024,1024]{1,0:T(8,128)(2,1)} fusion(f32[1024,1024]{1,0:T(8,128)} %get-tuple-element.29, f32[1024]{0:T(1024)S(1)} %get-tuple-element.27), kind=kLoop, calls=%fused_computation.17 | loop fusion | flops 4194304 | bytes 6295552 | tf_op jit(solution)/shard_map/convert_element_type | solution.py:16
  161.1 32.8 %all-reduce.6.cloned.1.call-done = bf16[1024,1024]{1,0:T(8,128)(2,1)} async-done(((bf16[1024,1024]{1,0:T(8,128)(2,1)}), bf16[1024,1024]{1,0:T(8,128)(2,1)}) %all-reduce.6.cloned.1.call-update) | async-done | bytes 2097168 | tf_op jit(solution)/shard_map/psum | solution.py:77
  193.9 0.0 all-reduce.8.cloned.1.call-update
  193.9 8.7 %subtract_convert_fusion.1 = bf16[1024,1024]{1,0:T(8,128)(2,1)} fusion(bf16[1024,1024]{1,0:T(8,128)(2,1)} %bitcast.14, bf16[1024,1024]{1,0:T(8,128)(2,1)} %fusion.7, bf16[1024,1024]{1,0:T(8,128)(2,1)} %get-tuple-element.28, s32[2048]{0:T(1024)S(1)} %add_select_fusion, s32[1024]{0:T(1024)S(1)} %eq.241), kind=kOutput, calls=%fused_computation.33 | convolution fusion | flops 4308598784 | bytes 8400896 | tf_op jit(solution)/shard_map/dot_general | solution.py:88
  202.6 0.0 all-to-all-done.4
  202.6 7.2 %all-to-all-start.5 = ((bf16[32,32,1024]{2,1,0:T(8,128)(2,1)}), bf16[32,32,1024]{2,1,0:T(8,128)(2,1)}, u32[]{:S(2)}, u32[]{:S(2)}) async-start(bf16[32,32,1024]{2,1,0:T(8,128)(2,1)} %bitcast.62), calls=%async_computation.5 | async-start | bytes 4194304 | tf_op jit(solution)/shard_map/all_to_all | solution.py:57
  209.9 45.0 %all-reduce.8.cloned.1.call-done = bf16[1024,1024]{1,0:T(8,128)(2,1)} async-done(((bf16[1024,1024]{1,0:T(8,128)(2,1)}), bf16[1024,1024]{1,0:T(8,128)(2,1)}) %all-reduce.8.cloned.1.call-update) | async-done | bytes 2097168 | tf_op jit(solution)/shard_map/psum | solution.py:77
  254.9 0.0 all-to-all-done.5
  254.9 5.9 %reduce-precision_convert_fusion = (bf16[1024,1024]{1,0:T(8,128)(2,1)S(1)}, bf16[1024,1024]{1,0:T(8,128)(2,1)S(1)}, f32[1024,1024]{1,0:T(8,128)}) fusion(f32[1024]{0:T(1024)S(1)} %get-tuple-element.26, f32[1024,1024]{1,0:T(8,128)} %get-tuple-element.29, bf16[1024,1024]{1,0:T(8,128)(2,1)} %all-reduce.6.cloned.1.call-done, f32[1024]{0:T(1024)S(1)} %get-tuple-element.25, ...), kind=kLoop, calls=%fused_computation.11 | loop fusion | flops 10485760 | bytes 16785408 | tf_op jit(solution)/shard_map/convert_element_type | solution.py:16
  260.8 7.0 %subtract_convert_fusion = bf16[1024,1024]{1,0:T(8,128)(2,1)} fusion(bf16[1024,1024]{1,0:T(8,128)(2,1)} %bitcast.16, bf16[1024,1024]{1,0:T(8,128)(2,1)S(1)} %get-tuple-element.31, bf16[1024,1024]{1,0:T(8,128)(2,1)S(1)} %get-tuple-element.30, s32[2048]{0:T(1024)S(1)} %add_select_fusion, s32[1024]{0:T(1024)S(1)} %eq.254), kind=kOutput, calls=%fused_computation.30 | convolution fusion | flops 4308598784 | bytes 8400896 | tf_op jit(solution)/shard_map/dot_general | solution.py:88
  267.8 7.5 %all-to-all-start.6 = ((bf16[32,32,1024]{2,1,0:T(8,128)(2,1)}), bf16[32,32,1024]{2,1,0:T(8,128)(2,1)}, u32[]{:S(2)}, u32[]{:S(2)}) async-start(bf16[32,32,1024]{2,1,0:T(8,128)(2,1)} %bitcast.64), calls=%async_computation.6 | async-start | bytes 4194304 | tf_op jit(solution)/shard_map/all_to_all | solution.py:57
  275.3 1.3 fusion.58
  276.6 2.9 fusion.59
  279.5 25.5 %all-to-all-done.6 = bf16[32,32,1024]{2,1,0:T(8,128)(2,1)} async-done(((bf16[32,32,1024]{2,1,0:T(8,128)(2,1)}), bf16[32,32,1024]{2,1,0:T(8,128)(2,1)}, u32[]{:S(2)}, u32[]{:S(2)}) %all-to-all-start.6) | async-done | bytes 2097184 | tf_op jit(solution)/shard_map/all_to_all | solution.py:57
  305.0 2.9 fusion.60
  307.9 2.0 pad_maximum_fusion
  (9 shorter events, 0.1 us)
Async XLA Ops:
  12.7 37.4 %all-to-all-start = ((bf16[32,32,1024]{2,1,0:T(8,128)(2,1)}), bf16[32,32,1024]{2,1,0:T(8,128)(2,1)S(1)}, u32[]{:S(2)}, u32[]{:S(2)}) async-start(bf16[32,32,1024]{2,1,0:T(8,128)(2,1)} %bitcast.63), calls=%async_computation | async-start | bytes 4194304 | tf_op jit(solution)/shard_map/all_to_all | solution.py:57
  50.1 11.1 %all-to-all-start.1 = ((s32[32,1,96]{2,1,0:T(1,128)}), s32[32,1,96]{2,1,0:T(1,128)S(1)}, u32[]{:S(2)}, u32[]{:S(2)}) async-start(s32[32,1,96]{2,1,0:T(1,128)} %bitcast.7), calls=%async_computation.1 | async-start | bytes 32768 | tf_op jit(solution)/shard_map/all_to_all | solution.py:43
  61.2 34.7 %all-to-all-start.2 = ((bf16[32,32,1024]{2,1,0:T(8,128)(2,1)}), bf16[32,32,1024]{2,1,0:T(8,128)(2,1)}, u32[]{:S(2)}, u32[]{:S(2)}) async-start(bf16[32,32,1024]{2,1,0:T(8,128)(2,1)} %bitcast.60), calls=%async_computation.2 | async-start | bytes 4194304 | tf_op jit(solution)/shard_map/all_to_all | solution.py:57
  66.0 66.7 %all-reduce.4.cloned.1.call-start = ((), (), s32[]{:S(2)}) async-start(), calls=%async_computation.7 | async-start | bytes 4194304 | tf_op jit(solution)/shard_map/psum | solution.py:77
  75.0 32.8 %copy-start = (s32[1024]{0:T(1024)S(1)}, s32[1024]{0:T(1024)}, u32[]{:S(2)}) copy-start(s32[1024]{0:T(1024)} %param.9) | copy-start | bytes 12292
  95.9 36.8 %all-to-all-start.3 = ((bf16[32,32,1024]{2,1,0:T(8,128)(2,1)}), bf16[32,32,1024]{2,1,0:T(8,128)(2,1)}, u32[]{:S(2)}, u32[]{:S(2)}) async-start(bf16[32,32,1024]{2,1,0:T(8,128)(2,1)} %bitcast.58), calls=%async_computation.3 | async-start | bytes 4194304 | tf_op jit(solution)/shard_map/all_to_all | solution.py:57
  100.7 93.2 %all-reduce.6.cloned.1.call-start = ((), (), s32[]{:S(2)}) async-start(), calls=%async_computation.8 | async-start | bytes 4194304 | tf_op jit(solution)/shard_map/psum | solution.py:77
  102.4 5.6 %collective-permute-start.2 = (s32[3,1024]{1,0:T(4,128)S(1)}, s32[3,1024]{1,0:T(4,128)S(1)}, u32[]{:S(2)}, u32[]{:S(2)}) collective-permute-start(s32[3,1024]{1,0:T(4,128)S(1)} %convert_reduce_fusion), channel_id=1, source_target_pairs={{0,96},{32,0},{64,32},{96,64},{1,97},{33,1},{65,33},{97,65},{2,98}... | collective-permute-start | bytes 36872 | tf_op jit(solution)/shard_map/ppermute | solution.py:51
  106.5 5.2 %collective-permute-start.1 = (s32[3,1024]{1,0:T(4,128)S(1)}, s32[3,1024]{1,0:T(4,128)S(1)}, u32[]{:S(2)}, u32[]{:S(2)}) collective-permute-start(s32[3,1024]{1,0:T(4,128)S(1)} %convert_reduce_fusion), channel_id=1, source_target_pairs={{0,64},{32,96},{64,0},{96,32},{1,65},{33,97},{65,1},{97,33},{2,66}... | collective-permute-start | bytes 36872 | tf_op jit(solution)/shard_map/ppermute | solution.py:51
  106.5 5.2 %collective-permute-start = (s32[3,1024]{1,0:T(4,128)S(1)}, s32[3,1024]{1,0:T(4,128)S(1)}, u32[]{:S(2)}, u32[]{:S(2)}) collective-permute-start(s32[3,1024]{1,0:T(4,128)S(1)} %convert_reduce_fusion), channel_id=1, source_target_pairs={{0,32},{32,64},{64,96},{96,0},{1,33},{33,65},{65,97},{97,1},{2,34}... | collective-permute-start | bytes 36872 | tf_op jit(solution)/shard_map/ppermute | solution.py:51
  144.0 58.6 %all-to-all-start.4 = ((bf16[32,32,1024]{2,1,0:T(8,128)(2,1)}), bf16[32,32,1024]{2,1,0:T(8,128)(2,1)S(1)}, u32[]{:S(2)}, u32[]{:S(2)}) async-start(bf16[32,32,1024]{2,1,0:T(8,128)(2,1)} %bitcast.61), calls=%async_computation.4 | async-start | bytes 4194304 | tf_op jit(solution)/shard_map/all_to_all | solution.py:57
  151.1 103.8 %all-reduce.8.cloned.1.call-start = ((), (), s32[]{:S(2)}) async-start(), calls=%async_computation.9 | async-start | bytes 4194304 | tf_op jit(solution)/shard_map/psum | solution.py:77
  202.6 52.3 %all-to-all-start.5 = ((bf16[32,32,1024]{2,1,0:T(8,128)(2,1)}), bf16[32,32,1024]{2,1,0:T(8,128)(2,1)}, u32[]{:S(2)}, u32[]{:S(2)}) async-start(bf16[32,32,1024]{2,1,0:T(8,128)(2,1)} %bitcast.62), calls=%async_computation.5 | async-start | bytes 4194304 | tf_op jit(solution)/shard_map/all_to_all | solution.py:57
  267.8 37.2 %all-to-all-start.6 = ((bf16[32,32,1024]{2,1,0:T(8,128)(2,1)}), bf16[32,32,1024]{2,1,0:T(8,128)(2,1)}, u32[]{:S(2)}, u32[]{:S(2)}) async-start(bf16[32,32,1024]{2,1,0:T(8,128)(2,1)} %bitcast.64), calls=%async_computation.6 | async-start | bytes 4194304 | tf_op jit(solution)/shard_map/all_to_all | solution.py:57
Sparse Core Ops, SparseCore 0:
  71.3 61.3 all-reduce.3
  135.2 58.6 all-reduce.5
  196.2 58.5 all-reduce.7
where the time goes:
time: 317 us; the launch traced here: 316 us
  waiting for transfers between devices  175 us (55%)
  matrix products  54.7 us (17%)
  starting transfers between devices  48.3 us (15%)
  other arithmetic  21.5 us (7%)
  between operations  13.9 us (4%)
    psum x3, waiting for transfers between devices, local(): totals.append(lax.psum(sums, 'grp'))  93.3 us
    all_to_all x6, waiting for transfers between devices, exchange(): rows = lax.all_to_all(rows, 'list', split_axis=0, concat_axis=0, tiled=True)  74.7 us
    all_to_all x6, starting transfers between devices, exchange(): rows = lax.all_to_all(rows, 'list', split_axis=0, concat_axis=0, tiled=True)  38.7 us
    dot_general x3, matrix products, local(): jnp.dot(one_hot.astype(jnp.bfloat16), split_table(current), preferred_ele...  21.6 us
    dot_general x3, matrix products, local(): sums = jnp.dot(one_hot, received[step], preferred_element_type=jnp.float32)  14.3 us
    dot_general x3, matrix products, local(): jnp.dot((dest[step][None, :] == row_iota[:, None]).astype(jnp.bfloat16),...  11.4 us
    convert_element_type x2, other arithmetic, split_table(): hi.astype(jnp.bfloat16)  11.3 us
    dot_general x3, matrix products, local(): jnp.dot(pick, back, preferred_element_type=jnp.float32).astype(jnp.bfloat16)  7.06 us
  transfers between devices with their start and end apart: 13, of which 8 were waited for; matrix products, arithmetic and copies ran while one was open for 18% of the time, Pallas kernels for 0%

commit v1 on v0

--- a/solution.py
+++ b/solution.py
@@ -74,7 +74,7 @@
         sums = sums.astype(jnp.bfloat16)
         if totals:
             sums = tie(sums, totals[-1])
-        totals.append(lax.psum(sums, "grp"))
+        totals.append(jnp.sum(lax.all_gather(sums, "grp"), axis=0))
     weights = counts.astype(jnp.float32)
     mass = weights[:, None] * centroids
     current = centroids

time: 317 us -> 400 us (1.26); the launches traced: 316 us -> 394 us
  waiting for transfers between devices: 175 us -> 241 us
  other arithmetic: 21.5 us -> 42.4 us
  matrix products: 54.7 us -> 48.5 us
    all_gather x0 -> x3, waiting for transfers between devices: none -> 99.5 us  [local(): totals.append(jnp.sum(lax.all_gather(sums, 'grp'), axis=0))]
    psum x3 -> x0, waiting for transfers between devices: 93.3 us -> none  [local(): totals.append(lax.psum(sums, 'grp'))]
    all_to_all x6, waiting for transfers between devices: 74.7 us -> 134 us  [exchange(): rows = lax.all_to_all(rows, 'list', split_axis=0, concat_axis=0, tiled=True)]
    reduce_sum x0 -> x3, other arithmetic: none -> 21.4 us  [local(): totals.append(jnp.sum(lax.all_gather(sums, 'grp'), axis=0))]
    all_to_all x6, starting transfers between devices: 38.7 us -> 31.9 us  [exchange(): rows = lax.all_to_all(rows, 'list', split_axis=0, concat_axis=0, tiled=True)]
  transfers between devices with their start and end apart: 13 -> 13, of which waited for: 8 -> 12; matrix products, arithmetic and copies ran while one was open for 18% -> 15% of each run, Pallas kernels for 0% -> 0%
where the time goes in v1:
time: 400 us; the launch traced here: 394 us
  waiting for transfers between devices  241 us (60%)
  matrix products  48.5 us (12%)
  starting transfers between devices  44.6 us (11%)
  other arithmetic  42.4 us (11%)
  between operations  14.2 us (4%)
    all_to_all x6, waiting for transfers between devices, exchange(): rows = lax.all_to_all(rows, 'list', split_axis=0, concat_axis=0, tiled=True)  134 us
    all_gather x3, waiting for transfers between devices, local(): totals.append(jnp.sum(lax.all_gather(sums, 'grp'), axis=0))  99.5 us
    all_to_all x6, starting transfers between devices, exchange(): rows = lax.all_to_all(rows, 'list', split_axis=0, concat_axis=0, tiled=True)  31.9 us
    reduce_sum x3, other arithmetic, local(): totals.append(jnp.sum(lax.all_gather(sums, 'grp'), axis=0))  21.4 us
    dot_general x3, matrix products, local(): jnp.dot(one_hot.astype(jnp.bfloat16), split_table(current), preferred_ele...  17.8 us
    convert_element_type x2, other arithmetic, split_table(): hi.astype(jnp.bfloat16)  11.9 us
    dot_general x3, matrix products, local(): jnp.dot((dest[step][None, :] == row_iota[:, None]).astype(jnp.bfloat16),...  11.4 us
    dot_general x3, matrix products, local(): sums = jnp.dot(one_hot, received[step], preferred_element_type=jnp.float32)  11 us
  transfers between devices with their start and end apart: 13, of which 12 were waited for; matrix products, arithmetic and copies ran while one was open for 15% of the time, Pallas kernels for 0%

profile of v1, /device:TPU:0, one launch (start us, length us, event | category | flops | bytes accessed | tf_op | source)
XLA Modules:
  0.0 393.6 jit_solution(9231359012911133353)
XLA Ops:
  7.2 0.7 copy.20
  7.9 0.3 fusion.62
  8.2 0.7 convert_add_fusion.2
  8.9 0.8 select_reduce_fusion
  9.7 0.1 sub.25
  9.9 0.7 reshape.93
  10.6 7.4 %all-to-all-start.1 = ((s32[32,1,96]{2,1,0:T(1,128)}), s32[32,1,96]{2,1,0:T(1,128)S(1)}, u32[]{:S(2)}, u32[]{:S(2)}) async-start(s32[32,1,96]{2,1,0:T(1,128)} %bitcast.7), calls=%async_computation.1 | async-start | bytes 32768 | tf_op jit(solution)/shard_map/all_to_all | solution.py:43
  18.0 3.8 fusion.39
  21.8 3.5 all-to-all-done.1
  25.2 4.0 %all-to-all-start = ((bf16[32,32,1024]{2,1,0:T(8,128)(2,1)}), bf16[32,32,1024]{2,1,0:T(8,128)(2,1)S(1)}, u32[]{:S(2)}, u32[]{:S(2)}) async-start(bf16[32,32,1024]{2,1,0:T(8,128)(2,1)} %bitcast.68), calls=%async_computation | async-start | bytes 4194304 | tf_op jit(solution)/shard_map/all_to_all | solution.py:57
  29.3 0.0 all-gather.7.cloned.1.call-start
  29.3 0.5 broadcast.53
  29.8 0.7 reduce.18
  30.5 0.1 reshape.94
  30.6 0.1 slice_reduce_fusion
  30.8 0.1 eq.226
  30.8 28.4 %all-to-all-done = bf16[32,32,1024]{2,1,0:T(8,128)(2,1)S(1)} async-done(((bf16[32,32,1024]{2,1,0:T(8,128)(2,1)}), bf16[32,32,1024]{2,1,0:T(8,128)(2,1)S(1)}, u32[]{:S(2)}, u32[]{:S(2)}) %all-to-all-start) | async-done | bytes 2097184 | tf_op jit(solution)/shard_map/all_to_all | solution.py:57
  59.2 3.7 fusion.42
  62.9 0.0 all-gather.7.cloned.1.call-update
  62.9 3.8 fusion.37
  66.7 4.0 %all-to-all-start.2 = ((bf16[32,32,1024]{2,1,0:T(8,128)(2,1)}), bf16[32,32,1024]{2,1,0:T(8,128)(2,1)S(1)}, u32[]{:S(2)}, u32[]{:S(2)}) async-start(bf16[32,32,1024]{2,1,0:T(8,128)(2,1)} %bitcast.74), calls=%async_computation.2 | async-start | bytes 4194304 | tf_op jit(solution)/shard_map/all_to_all | solution.py:57
  70.8 0.4 all-gather.9.cloned.1.call-start
  71.1 0.1 eq.241
  71.2 29.5 %all-to-all-done.2 = bf16[32,32,1024]{2,1,0:T(8,128)(2,1)S(1)} async-done(((bf16[32,32,1024]{2,1,0:T(8,128)(2,1)}), bf16[32,32,1024]{2,1,0:T(8,128)(2,1)S(1)}, u32[]{:S(2)}, u32[]{:S(2)}) %all-to-all-start.2) | async-done | bytes 2097184 | tf_op jit(solution)/shard_map/all_to_all | solution.py:57
  100.7 3.7 fusion.41
  104.4 40.1 %all-gather.7.cloned.1.call-done = bf16[4096,1024]{1,0:T(8,128)(2,1)} async-done(((bf16[1024,1024]{1,0:T(8,128)(2,1)}), bf16[4096,1024]{1,0:T(8,128)(2,1)}) %all-gather.7.cloned.1.call-update) | async-done | bytes 8388624 | tf_op jit(solution)/shard_map/all_gather | solution.py:77
  144.5 7.4 %reduce_sum.65 = bf16[1024,1024]{1,0:T(8,128)(2,1)} reduce(bf16[4,1024,1024]{2,1,0:T(8,128)(2,1)} %bitcast.61, bf16[]{:T(256)} %constant.35.clone.1), dimensions={0}, to_apply=%region_2.3 | reduce | flops 3145728 | bytes 10485762 | tf_op jit(solution)/shard_map/reduce_sum | solution.py:77
  151.9 0.0 all-gather.9.cloned.1.call-update
  151.9 3.8 fusion.38
  155.7 7.1 %all-to-all-start.3 = ((bf16[32,32,1024]{2,1,0:T(8,128)(2,1)}), bf16[32,32,1024]{2,1,0:T(8,128)(2,1)S(1)}, u32[]{:S(2)}, u32[]{:S(2)}) async-start(bf16[32,32,1024]{2,1,0:T(8,128)(2,1)} %bitcast.73), calls=%async_computation.3 | async-start | bytes 4194304 | tf_op jit(solution)/shard_map/all_to_all | solution.py:57
  162.8 0.6 all-gather.11.cloned.1.call-start
  163.5 0.1 eq.254
  163.5 29.3 %all-to-all-done.3 = bf16[32,32,1024]{2,1,0:T(8,128)(2,1)S(1)} async-done(((bf16[32,32,1024]{2,1,0:T(8,128)(2,1)}), bf16[32,32,1024]{2,1,0:T(8,128)(2,1)S(1)}, u32[]{:S(2)}, u32[]{:S(2)}) %all-to-all-start.3) | async-done | bytes 2097184 | tf_op jit(solution)/shard_map/all_to_all | solution.py:57
  192.8 3.7 fusion.40
  196.5 39.7 %all-gather.9.cloned.1.call-done = bf16[4096,1024]{1,0:T(8,128)(2,1)} async-done(((bf16[1024,1024]{1,0:T(8,128)(2,1)}), bf16[4096,1024]{1,0:T(8,128)(2,1)}) %all-gather.9.cloned.1.call-update) | async-done | bytes 8388624 | tf_op jit(solution)/shard_map/all_gather | solution.py:77
  236.2 6.5 %reduce_sum.67 = bf16[1024,1024]{1,0:T(8,128)(2,1)S(1)} reduce(bf16[4,1024,1024]{2,1,0:T(8,128)(2,1)} %bitcast.60, bf16[]{:T(256)} %constant.35.clone.1), dimensions={0}, to_apply=%region_4.5 | reduce | flops 3145728 | bytes 10485762 | tf_op jit(solution)/shard_map/reduce_sum | solution.py:77
  242.7 0.0 all-gather.11.cloned.1.call-update
  242.8 0.1 eq.247
  242.9 1.5 convert_reduce_fusion
  244.4 1.3 collective-permute-start.2
  245.8 2.2 collective-permute-start.1
  247.9 0.8 collective-permute-start
  248.8 0.0 collective-permute-done.2
  248.8 2.2 collective-permute-done.1
  251.0 2.0 collective-permute-done
  253.1 6.2 %reduce-precision_convert_fusion.1 = (bf16[1024,1024]{1,0:T(8,128)(2,1)}, f32[1024,1024]{1,0:T(8,128)}, bf16[1024,1024]{1,0:T(8,128)(2,1)S(1)}, bf16[1024,1024]{1,0:T(8,128)(2,1)S(1)}) fusion(f32[1024]{0:T(1024)S(1)} %get-tuple-element.27, bf16[1024,1024]{1,0:T(8,128)(2,1)} %reduce_sum.65, f32[1024,1024]{1,0:T(8,128)} %param.8, ...), kind=kLoop, calls=%fused_computation.13 | loop fusion | flops 10485760 | bytes 16785408 | tf_op jit(solution)/shard_map/convert_element_type | solution.py:16
  259.3 5.9 %subtract_convert_fusion.2 = bf16[1024,1024]{1,0:T(8,128)(2,1)} fusion(bf16[1024,1024]{1,0:T(8,128)(2,1)S(1)} %bitcast.63, bf16[1024,1024]{1,0:T(8,128)(2,1)S(1)} %get-tuple-element.34, bf16[1024,1024]{1,0:T(8,128)(2,1)S(1)} %get-tuple-element.33, s32[2048]{0:T(1024)S(1)} %add_select_fusion, s32[1024]{0:T(1024)S(1)} %eq.226), kind=kOutput, calls=%fused_computation.36 | convolution fusion | flops 4308598784 | bytes 8400896 | tf_op jit(solution)/shard_map/dot_general | solution.py:88
  265.2 7.2 %all-to-all-start.4 = ((bf16[32,32,1024]{2,1,0:T(8,128)(2,1)}), bf16[32,32,1024]{2,1,0:T(8,128)(2,1)}, u32[]{:S(2)}, u32[]{:S(2)}) async-start(bf16[32,32,1024]{2,1,0:T(8,128)(2,1)} %bitcast.70), calls=%async_computation.4 | async-start | bytes 4194304 | tf_op jit(solution)/shard_map/all_to_all | solution.py:57
  272.5 3.3 fusion.7
  275.8 0.3 copy-done.6
  276.1 5.9 %subtract_convert_fusion.1 = bf16[1024,1024]{1,0:T(8,128)(2,1)} fusion(bf16[1024,1024]{1,0:T(8,128)(2,1)S(1)} %bitcast.67, bf16[1024,1024]{1,0:T(8,128)(2,1)S(1)} %fusion.7, bf16[1024,1024]{1,0:T(8,128)(2,1)S(1)} %copy-done.6, s32[2048]{0:T(1024)S(1)} %add_select_fusion, s32[1024]{0:T(1024)S(1)} %eq.241), kind=kOutput, calls=%fused_computation.33 | convolution fusion | flops 4308598784 | bytes 8400896 | tf_op jit(solution)/shard_map/dot_general | solution.py:88
  282.0 20.5 %all-to-all-done.4 = bf16[32,32,1024]{2,1,0:T(8,128)(2,1)} async-done(((bf16[32,32,1024]{2,1,0:T(8,128)(2,1)}), bf16[32,32,1024]{2,1,0:T(8,128)(2,1)}, u32[]{:S(2)}, u32[]{:S(2)}) %all-to-all-start.4) | async-done | bytes 2097184 | tf_op jit(solution)/shard_map/all_to_all | solution.py:57
  302.4 5.0 %all-to-all-start.5 = ((bf16[32,32,1024]{2,1,0:T(8,128)(2,1)}), bf16[32,32,1024]{2,1,0:T(8,128)(2,1)}, u32[]{:S(2)}, u32[]{:S(2)}) async-start(bf16[32,32,1024]{2,1,0:T(8,128)(2,1)} %bitcast.69), calls=%async_computation.5 | async-start | bytes 4194304 | tf_op jit(solution)/shard_map/all_to_all | solution.py:57
  307.4 19.7 %all-gather.11.cloned.1.call-done = bf16[4096,1024]{1,0:T(8,128)(2,1)} async-done(((bf16[1024,1024]{1,0:T(8,128)(2,1)}), bf16[4096,1024]{1,0:T(8,128)(2,1)}) %all-gather.11.cloned.1.call-update) | async-done | bytes 8388624 | tf_op jit(solution)/shard_map/all_gather | solution.py:77
  327.1 7.5 %reduce_sum.68 = bf16[1024,1024]{1,0:T(8,128)(2,1)} reduce(bf16[4,1024,1024]{2,1,0:T(8,128)(2,1)} %bitcast.59, bf16[]{:T(256)} %constant.35.clone.1), dimensions={0}, to_apply=%region_5.6 | reduce | flops 3145728 | bytes 10485762 | tf_op jit(solution)/shard_map/reduce_sum | solution.py:77
  334.6 2.8 all-to-all-done.5
  337.4 5.7 %reduce-precision_convert_fusion = (bf16[1024,1024]{1,0:T(8,128)(2,1)S(1)}, bf16[1024,1024]{1,0:T(8,128)(2,1)S(1)}, f32[1024,1024]{1,0:T(8,128)}) fusion(f32[1024]{0:T(1024)S(1)} %get-tuple-element.26, f32[1024,1024]{1,0:T(8,128)} %get-tuple-element.29, bf16[1024,1024]{1,0:T(8,128)(2,1)S(1)} %reduce_sum.67, f32[1024]{0:T(1024)S(1)} %get-tuple-element.25, ...), kind=kLoop, calls=%fused_computation.11 | loop fusion | flops 10485760 | bytes 16785408 | tf_op jit(solution)/shard_map/convert_element_type | solution.py:16
  343.1 5.9 %subtract_convert_fusion = bf16[1024,1024]{1,0:T(8,128)(2,1)} fusion(bf16[1024,1024]{1,0:T(8,128)(2,1)S(1)} %bitcast.65, bf16[1024,1024]{1,0:T(8,128)(2,1)S(1)} %get-tuple-element.31, bf16[1024,1024]{1,0:T(8,128)(2,1)S(1)} %get-tuple-element.30, s32[2048]{0:T(1024)S(1)} %add_select_fusion, s32[1024]{0:T(1024)S(1)} %eq.254), kind=kOutput, calls=%fused_computation.30 | convolution fusion | flops 4308598784 | bytes 8400896 | tf_op jit(solution)/shard_map/dot_general | solution.py:88
  349.0 4.5 %all-to-all-start.6 = ((bf16[32,32,1024]{2,1,0:T(8,128)(2,1)}), bf16[32,32,1024]{2,1,0:T(8,128)(2,1)S(1)}, u32[]{:S(2)}, u32[]{:S(2)}) async-start(bf16[32,32,1024]{2,1,0:T(8,128)(2,1)} %bitcast.72), calls=%async_computation.6 | async-start | bytes 4194304 | tf_op jit(solution)/shard_map/all_to_all | solution.py:57
  353.6 2.9 fusion.58
  356.4 3.9 fusion.59
  360.3 23.2 %all-to-all-done.6 = bf16[32,32,1024]{2,1,0:T(8,128)(2,1)S(1)} async-done(((bf16[32,32,1024]{2,1,0:T(8,128)(2,1)}), bf16[32,32,1024]{2,1,0:T(8,128)(2,1)S(1)}, u32[]{:S(2)}, u32[]{:S(2)}) %all-to-all-start.6) | async-done | bytes 2097184 | tf_op jit(solution)/shard_map/all_to_all | solution.py:57
  383.5 1.3 fusion.60
  384.8 2.0 pad_maximum_fusion
  (26 shorter events, 0.1 us)
Async XLA Ops:
  10.6 14.7 %all-to-all-start.1 = ((s32[32,1,96]{2,1,0:T(1,128)}), s32[32,1,96]{2,1,0:T(1,128)S(1)}, u32[]{:S(2)}, u32[]{:S(2)}) async-start(s32[32,1,96]{2,1,0:T(1,128)} %bitcast.7), calls=%async_computation.1 | async-start | bytes 32768 | tf_op jit(solution)/shard_map/all_to_all | solution.py:43
  25.2 34.0 %all-to-all-start = ((bf16[32,32,1024]{2,1,0:T(8,128)(2,1)}), bf16[32,32,1024]{2,1,0:T(8,128)(2,1)S(1)}, u32[]{:S(2)}, u32[]{:S(2)}) async-start(bf16[32,32,1024]{2,1,0:T(8,128)(2,1)} %bitcast.68), calls=%async_computation | async-start | bytes 4194304 | tf_op jit(solution)/shard_map/all_to_all | solution.py:57
  29.3 115.2 %all-gather.7.cloned.1.call-start = ((), (), s32[]{:S(2)}) async-start(), calls=%async_computation.7 | async-start | bytes 10485760 | tf_op jit(solution)/shard_map/all_gather | solution.py:77
  59.2 3.7 copy-start
  66.7 34.0 %all-to-all-start.2 = ((bf16[32,32,1024]{2,1,0:T(8,128)(2,1)}), bf16[32,32,1024]{2,1,0:T(8,128)(2,1)S(1)}, u32[]{:S(2)}, u32[]{:S(2)}) async-start(bf16[32,32,1024]{2,1,0:T(8,128)(2,1)} %bitcast.74), calls=%async_computation.2 | async-start | bytes 4194304 | tf_op jit(solution)/shard_map/all_to_all | solution.py:57
  70.8 165.5 %all-gather.9.cloned.1.call-start = ((), (), s32[]{:S(2)}) async-start(), calls=%async_computation.8 | async-start | bytes 10485760 | tf_op jit(solution)/shard_map/all_gather | solution.py:77
  100.7 3.7 copy-start.4
  155.7 37.1 %all-to-all-start.3 = ((bf16[32,32,1024]{2,1,0:T(8,128)(2,1)}), bf16[32,32,1024]{2,1,0:T(8,128)(2,1)S(1)}, u32[]{:S(2)}, u32[]{:S(2)}) async-start(bf16[32,32,1024]{2,1,0:T(8,128)(2,1)} %bitcast.73), calls=%async_computation.3 | async-start | bytes 4194304 | tf_op jit(solution)/shard_map/all_to_all | solution.py:57
  162.8 164.3 %all-gather.11.cloned.1.call-start = ((), (), s32[]{:S(2)}) async-start(), calls=%async_computation.9 | async-start | bytes 10485760 | tf_op jit(solution)/shard_map/all_gather | solution.py:77
  192.8 3.7 copy-start.2
  236.2 12.5 %copy-start.8 = (s32[1024]{0:T(1024)S(1)}, s32[1024]{0:T(1024)}, u32[]{:S(2)}) copy-start(s32[1024]{0:T(1024)} %param.9) | copy-start | bytes 12292
  244.4 4.3 %collective-permute-start.2 = (s32[3,1024]{1,0:T(4,128)S(1)}, s32[3,1024]{1,0:T(4,128)S(1)}, u32[]{:S(2)}, u32[]{:S(2)}) collective-permute-start(s32[3,1024]{1,0:T(4,128)S(1)} %convert_reduce_fusion), channel_id=1, source_target_pairs={{0,96},{32,0},{64,32},{96,64},{1,97},{33,1},{65,33},{97,65},{2,98}... | collective-permute-start | bytes 36872 | tf_op jit(solution)/shard_map/ppermute | solution.py:51
  245.8 5.2 %collective-permute-start.1 = (s32[3,1024]{1,0:T(4,128)S(1)}, s32[3,1024]{1,0:T(4,128)S(1)}, u32[]{:S(2)}, u32[]{:S(2)}) collective-permute-start(s32[3,1024]{1,0:T(4,128)S(1)} %convert_reduce_fusion), channel_id=1, source_target_pairs={{0,64},{32,96},{64,0},{96,32},{1,65},{33,97},{65,1},{97,33},{2,66}... | collective-permute-start | bytes 36872 | tf_op jit(solution)/shard_map/ppermute | solution.py:51
  247.9 5.1 %collective-permute-start = (s32[3,1024]{1,0:T(4,128)S(1)}, s32[3,1024]{1,0:T(4,128)S(1)}, u32[]{:S(2)}, u32[]{:S(2)}) collective-permute-start(s32[3,1024]{1,0:T(4,128)S(1)} %convert_reduce_fusion), channel_id=1, source_target_pairs={{0,32},{32,64},{64,96},{96,0},{1,33},{33,65},{65,97},{97,1},{2,34}... | collective-permute-start | bytes 36872 | tf_op jit(solution)/shard_map/ppermute | solution.py:51
  253.1 6.2 %copy-start.1 = (bf16[32,32,1024]{2,1,0:T(8,128)(2,1)S(1)}, bf16[32,32,1024]{2,1,0:T(8,128)(2,1)}, u32[]{:S(2)}) copy-start(bf16[32,32,1024]{2,1,0:T(8,128)(2,1)} %copy-done) | copy-start | bytes 6291460
  265.2 37.2 %all-to-all-start.4 = ((bf16[32,32,1024]{2,1,0:T(8,128)(2,1)}), bf16[32,32,1024]{2,1,0:T(8,128)(2,1)}, u32[]{:S(2)}, u32[]{:S(2)}) async-start(bf16[32,32,1024]{2,1,0:T(8,128)(2,1)} %bitcast.70), calls=%async_computation.4 | async-start | bytes 4194304 | tf_op jit(solution)/shard_map/all_to_all | solution.py:57
  272.5 3.3 copy-start.5
  272.5 3.6 copy-start.6
  302.4 34.9 %all-to-all-start.5 = ((bf16[32,32,1024]{2,1,0:T(8,128)(2,1)}), bf16[32,32,1024]{2,1,0:T(8,128)(2,1)}, u32[]{:S(2)}, u32[]{:S(2)}) async-start(bf16[32,32,1024]{2,1,0:T(8,128)(2,1)} %bitcast.69), calls=%async_computation.5 | async-start | bytes 4194304 | tf_op jit(solution)/shard_map/all_to_all | solution.py:57
  337.4 5.7 %copy-start.3 = (bf16[32,32,1024]{2,1,0:T(8,128)(2,1)S(1)}, bf16[32,32,1024]{2,1,0:T(8,128)(2,1)}, u32[]{:S(2)}) copy-start(bf16[32,32,1024]{2,1,0:T(8,128)(2,1)} %copy-done.2) | copy-start | bytes 6291460
  349.0 34.5 %all-to-all-start.6 = ((bf16[32,32,1024]{2,1,0:T(8,128)(2,1)}), bf16[32,32,1024]{2,1,0:T(8,128)(2,1)S(1)}, u32[]{:S(2)}, u32[]{:S(2)}) async-start(bf16[32,32,1024]{2,1,0:T(8,128)(2,1)} %bitcast.72), calls=%async_computation.6 | async-start | bytes 4194304 | tf_op jit(solution)/shard_map/all_to_all | solution.py:57
  383.5 1.3 copy-start.7
Sparse Core Ops, SparseCore 0:
  63.0 81.3 all-gather.6
  152.0 84.1 all-gather.8
  242.9 84.1 all-gather.10
